TPU v7x, 32 devices: a whole 2x2x4 slice. The times are simulated.
32 devices in a mesh: gx: 8 (over z, y), gy: 4 (over x, core).
Axes of the slice: x: 2, y: 2, z: 4, core: 2. Of those that a mesh axis runs over, the one named last changes fastest.
Arguments:
- layer_in: bfloat16 [2048, 1536], P('gx', 'gy'), may hold values from -40 to 40
- first_gain: float32 [1536], P('gy'), may hold values from 0.5 to 1.5
- query_weight: bfloat16 [1536, 1536], P('gx', 'gy'), may hold values from -0.21875 to 0.21875
- key_matrix: bfloat16 [1536, 768], P('gx', 'gy'), may hold values from -0.21875 to 0.21875
- value_matrix: bfloat16 [1536, 768], P('gx', 'gy'), may hold values from -0.15625 to 0.15625
- out_weight: bfloat16 [1536, 1536], P('gy', 'gx'), may hold values from -0.875 to 0.875
- second_gain: float32 [1536], P('gy'), may hold values from 0.5 to 1.5
- gate_weight: bfloat16 [1536, 4096], P('gx', 'gy'), may hold values from -0.15625 to 0.15625
- up_weight: bfloat16 [1536, 4096], P('gx', 'gy'), may hold values from -0.15625 to 0.15625
- down_weight: bfloat16 [4096, 1536], P('gy', 'gx'), may hold values from -0.1875 to 0.1875
- out_grad: bfloat16 [2048, 1536], P('gx', 'gy'), may hold values from -6 to 6
Outputs:
- layer_out: bfloat16 [2048, 1536], P('gx', 'gy')
- in_grad: float32 [2048, 1536], P('gx', 'gy')
- first_gain_grad: float32 [1536], P('gy')
- query_grad: float32 [1536, 1536], P('gx', 'gy')
- key_grad: float32 [1536, 768], P('gx', 'gy')
- value_grad: float32 [1536, 768], P('gx', 'gy')
- out_proj_grad: float32 [1536, 1536], P('gy', 'gx')
- second_gain_grad: float32 [1536], P('gy')
- gate_grad: float32 [1536, 4096], P('gx', 'gy')
- up_grad: float32 [1536, 4096], P('gx', 'gy')
- down_grad: float32 [4096, 1536], P('gy', 'gx')
All inputs are finite; a program needn't handle non-finite values.
Results may differ from a plain program's by a relative error of at most 0.024.
Values may be sent and summed in bfloat16 or wider, within the bound.
No kernel may reach another device: no remote copies, remote signals or barrier semaphores. Data moves between devices by JAX's collectives and lax.ppermute only.
A program may use at most 128 MiB of HBM per device.

v0:
```python
from functools import partial

import jax
import jax.numpy as jnp
from jax import lax
from jax.sharding import PartitionSpec as P

HEAD_DIM = 96
PROMPT_DEV = 4
CONT_DEV = 4


eps = 1e-05
neg_big = -1e30
rope_base = 100000.0


def from_behind(value, axis, steps):
    count = lax.axis_size(axis)
    leading, last = (max(0, -steps), min(count, count - steps))
    return lax.ppermute(value, axis, [(source, source + steps) for source in range(leading, last)])


def rope_tables(positions, half):
    freq = rope_base ** (-(2.0 * jnp.arange(half, dtype=jnp.float32)) / (2.0 * half))
    angle = positions.astype(jnp.float32)[:, None] * freq[None, :]
    return (jnp.cos(angle), jnp.sin(angle))


def apply_rotary(values, cosine_table, sine_table, sign):
    half = values.shape[-1] // 2
    first = values[..., :half]
    second = values[..., half:]
    cos_part = cosine_table[:, None, :]
    sin_part = sine_table[:, None, :] * sign
    return jnp.concatenate(
        [first * cos_part - second * sin_part, second * cos_part + first * sin_part], axis=-1
    )


def dot_last(left, right):
    return lax.dot_general(
        left, right, (((1,), (1,)), ((), ())), preferred_element_type=jnp.float32
    )


def dot_first(left, right):
    return lax.dot_general(
        left, right, (((0,), (0,)), ((), ())), preferred_element_type=jnp.float32
    )


def norm_forward(local_rows, gain, model_width):
    squares = lax.psum(jnp.sum(local_rows * local_rows, axis=1), "gy")
    inverse = lax.rsqrt(squares / model_width + eps)
    normed = (local_rows * inverse[:, None] * gain[None, :]).astype(jnp.bfloat16)
    return (inverse, lax.all_gather(normed, "gy", axis=1, tiled=True))


def norm_backward(local_rows, inverse, gain, normed_grad, model_width):
    scaled = normed_grad * gain[None, :]
    gain_term = jnp.sum(normed_grad * local_rows * inverse[:, None], axis=0)
    inner = lax.psum(jnp.sum(scaled * local_rows, axis=1), "gy")
    local_grad = (
        inverse[:, None] * scaled - local_rows * (inverse**3 * inner / model_width)[:, None]
    )
    return (local_grad, gain_term)


def sum_heads(partial_rows):
    return lax.psum_scatter(
        partial_rows.astype(jnp.bfloat16), "gy", scatter_dimension=1, tiled=True
    ).astype(jnp.float32)


def spread_grad(grad_rows):
    return lax.all_gather(grad_rows.astype(jnp.bfloat16), "gy", axis=1, tiled=True)


def sum_normed(partial_rows):
    return lax.psum_scatter(
        partial_rows.astype(jnp.bfloat16), "gy", scatter_dimension=1, tiled=True
    ).astype(jnp.float32)


def keep_carried(carried):
    return carried


def fold_block(carried, query_rows, key_rows, value_rows, allowed, score_scale):
    row_max, row_total, weighted = carried
    head_size = query_rows.shape[-1]
    split_keys = key_rows.reshape(key_rows.shape[0], -1, head_size)
    split_values = value_rows.reshape(value_rows.shape[0], -1, head_size)
    scores = (
        jnp.einsum("tkgd,skd->kgts", query_rows, split_keys, preferred_element_type=jnp.float32)
        * score_scale
    )
    if allowed is not None:
        scores = jnp.where(allowed, scores, neg_big)
    new_max = jnp.maximum(row_max, jnp.max(scores, axis=-1))
    rescale = jnp.exp(row_max - new_max)
    weights = jnp.exp(scores - new_max[..., None])
    row_total = row_total * rescale + jnp.sum(weights, axis=-1)
    weighted = weighted * rescale[..., None] + jnp.einsum(
        "kgts,skd->kgtd",
        weights.astype(jnp.bfloat16),
        split_values,
        preferred_element_type=jnp.float32,
    )
    return (new_max, row_total, weighted)


def block_grads(
    query_rows, key_rows, value_rows, rows_grad, log_total, row_delta, allowed, score_scale
):
    head_size = query_rows.shape[-1]
    key_count = key_rows.shape[0]
    split_keys = key_rows.reshape(key_count, -1, head_size)
    split_values = value_rows.reshape(key_count, -1, head_size)
    scores = (
        jnp.einsum("tkgd,skd->kgts", query_rows, split_keys, preferred_element_type=jnp.float32)
        * score_scale
    )
    prob_rows = jnp.exp(scores - log_total[..., None])
    if allowed is not None:
        prob_rows = jnp.where(allowed, prob_rows, 0.0)
    value_part = jnp.einsum(
        "kgts,tkgd->skd",
        prob_rows.astype(jnp.bfloat16),
        rows_grad,
        preferred_element_type=jnp.float32,
    )
    prob_grad = jnp.einsum(
        "tkgd,skd->kgts", rows_grad, split_values, preferred_element_type=jnp.float32
    )
    score_grad = (prob_rows * (prob_grad - row_delta[..., None])).astype(jnp.bfloat16)
    query_part = (
        jnp.einsum("kgts,skd->tkgd", score_grad, split_keys, preferred_element_type=jnp.float32)
        * score_scale
    )
    key_part = (
        jnp.einsum("kgts,tkgd->skd", score_grad, query_rows, preferred_element_type=jnp.float32)
        * score_scale
    )
    return (query_part, key_part.reshape(key_count, -1), value_part.reshape(key_count, -1))


def shards(
    layer_in,
    first_gain,
    query_weight,
    key_matrix,
    value_matrix,
    out_weight,
    second_gain,
    gate_weight,
    up_weight,
    down_weight,
    out_grad,
):
    tok_rows = layer_in.shape[0]
    model_width = layer_in.shape[1] * lax.axis_size("gy")
    heads_dev = query_weight.shape[1] // HEAD_DIM
    kv_dev = key_matrix.shape[1] // HEAD_DIM
    per_kv = heads_dev // kv_dev
    score_scale = HEAD_DIM ** (-0.5)
    group_len = PROMPT_DEV + CONT_DEV
    device_place = lax.axis_index("gx")
    offset = device_place % group_len
    within = jnp.arange(tok_rows, dtype=jnp.int32)
    positions = jnp.where(
        offset < PROMPT_DEV, offset * tok_rows + within, PROMPT_DEV * tok_rows + within
    )
    cosine_table, sine_table = rope_tables(positions, HEAD_DIM // 2)
    causal = within[:, None] >= within[None, :]
    query_full, key_full, value_full, out_full = (
        lax.all_gather(query_weight, "gx", axis=0, tiled=True),
        lax.all_gather(key_matrix, "gx", axis=0, tiled=True),
        lax.all_gather(value_matrix, "gx", axis=0, tiled=True),
        lax.all_gather(out_weight, "gx", axis=1, tiled=True),
    )
    gate_full, up_full, down_full = (
        lax.all_gather(gate_weight, "gx", axis=0, tiled=True),
        lax.all_gather(up_weight, "gx", axis=0, tiled=True),
        lax.all_gather(down_weight, "gx", axis=1, tiled=True),
    )
    input_rows = layer_in.astype(jnp.float32)
    inverse_in, normed_in = norm_forward(input_rows, first_gain, model_width)
    query_pre = jnp.dot(normed_in, query_full, preferred_element_type=jnp.float32)
    key_pre = jnp.dot(normed_in, key_full, preferred_element_type=jnp.float32)
    value_pre = jnp.dot(normed_in, value_full, preferred_element_type=jnp.float32)
    query_rot = apply_rotary(
        query_pre.reshape(tok_rows, heads_dev, HEAD_DIM), cosine_table, sine_table, 1.0
    ).astype(jnp.bfloat16)
    query_rot = query_rot.reshape(tok_rows, kv_dev, per_kv, HEAD_DIM)
    key_rot = apply_rotary(
        key_pre.reshape(tok_rows, kv_dev, HEAD_DIM), cosine_table, sine_table, 1.0
    ).astype(jnp.bfloat16)
    key_rot = key_rot.reshape(tok_rows, kv_dev * HEAD_DIM)
    value_low = value_pre.astype(jnp.bfloat16)
    remote = []
    for distance in range(1, group_len):
        arrived = from_behind((key_rot, value_low), "gx", distance)
        remote.append(
            (arrived[0], arrived[1], (offset >= distance) & (offset - distance < PROMPT_DEV))
        )
    carried = (
        jnp.full((kv_dev, per_kv, tok_rows), neg_big, jnp.float32),
        jnp.zeros((kv_dev, per_kv, tok_rows), jnp.float32),
        jnp.zeros((kv_dev, per_kv, tok_rows, HEAD_DIM), jnp.float32),
    )
    carried = fold_block(carried, query_rot, key_rot, value_low, causal, score_scale)
    for key_far, value_far, needed in remote:
        carried = lax.cond(
            needed,
            partial(
                fold_block,
                query_rows=query_rot,
                key_rows=key_far,
                value_rows=value_far,
                allowed=None,
                score_scale=score_scale,
            ),
            keep_carried,
            carried,
        )
    row_max, row_total, weighted = carried
    log_total = row_max + jnp.log(row_total)
    attended_rows = jnp.transpose(weighted / row_total[..., None], (2, 0, 1, 3))
    attended_low = attended_rows.reshape(tok_rows, heads_dev * HEAD_DIM).astype(jnp.bfloat16)
    hidden_rows = input_rows + sum_heads(
        jnp.dot(attended_low, out_full, preferred_element_type=jnp.float32)
    )
    inverse_mid, normed_mid = norm_forward(hidden_rows, second_gain, model_width)
    gate_pre = jnp.dot(normed_mid, gate_full, preferred_element_type=jnp.float32)
    up_pre = jnp.dot(normed_mid, up_full, preferred_element_type=jnp.float32)
    active = (jax.nn.silu(gate_pre) * up_pre).astype(jnp.bfloat16)
    layer_out = (
        hidden_rows + sum_heads(jnp.dot(active, down_full, preferred_element_type=jnp.float32))
    ).astype(jnp.bfloat16)
    grad_rows = out_grad.astype(jnp.float32)
    mlp_grad = spread_grad(grad_rows)
    down_full_grad = dot_first(active, mlp_grad)
    active_grad = dot_last(mlp_grad, down_full)
    sigmoid_gate = jax.nn.sigmoid(gate_pre)
    gate_low = (
        active_grad * up_pre * sigmoid_gate * (1.0 + gate_pre * (1.0 - sigmoid_gate))
    ).astype(jnp.bfloat16)
    up_low = (active_grad * gate_pre * sigmoid_gate).astype(jnp.bfloat16)
    gate_full_grad = dot_first(normed_mid, gate_low)
    up_full_grad = dot_first(normed_mid, up_low)
    normed_mid_grad = sum_normed(dot_last(gate_low, gate_full) + dot_last(up_low, up_full))
    mid_term, second_term = norm_backward(
        hidden_rows, inverse_mid, second_gain, normed_mid_grad, model_width
    )
    grad_rows = grad_rows + mid_term
    attn_grad = spread_grad(grad_rows)
    out_full_grad = dot_first(attended_low, attn_grad)
    attended_grad = (
        dot_last(attn_grad, out_full)
        .astype(jnp.bfloat16)
        .reshape(tok_rows, kv_dev, per_kv, HEAD_DIM)
    )
    row_delta = jnp.einsum("tkgd,tkgd->kgt", attended_grad.astype(jnp.float32), attended_rows)
    query_acc, key_acc, value_acc = block_grads(
        query_rot, key_rot, value_low, attended_grad, log_total, row_delta, causal, score_scale
    )
    zero_grads = (jnp.zeros_like(query_acc), jnp.zeros_like(key_acc), jnp.zeros_like(value_acc))

    def empty_grads():
        return zero_grads

    far_grads = []
    for key_far, value_far, needed in remote:
        grad_parts = lax.cond(
            needed,
            partial(
                block_grads,
                query_rot,
                key_far,
                value_far,
                attended_grad,
                log_total,
                row_delta,
                None,
                score_scale,
            ),
            empty_grads,
        )
        query_acc = query_acc + grad_parts[0]
        far_grads.append((grad_parts[1], grad_parts[2]))
    for index_far, (key_part, value_part) in enumerate(far_grads):
        returned = (
            from_behind(key_part.astype(jnp.bfloat16), "gx", -(index_far + 1)).astype(
                key_part.dtype
            ),
            from_behind(value_part.astype(jnp.bfloat16), "gx", -(index_far + 1)).astype(
                value_part.dtype
            ),
        )
        key_acc = key_acc + returned[0]
        value_acc = value_acc + returned[1]
    query_low = apply_rotary(
        query_acc.reshape(tok_rows, heads_dev, HEAD_DIM), cosine_table, sine_table, -1.0
    ).astype(jnp.bfloat16)
    query_low = query_low.reshape(tok_rows, heads_dev * HEAD_DIM)
    key_low = apply_rotary(
        key_acc.reshape(tok_rows, kv_dev, HEAD_DIM), cosine_table, sine_table, -1.0
    ).astype(jnp.bfloat16)
    key_low = key_low.reshape(tok_rows, kv_dev * HEAD_DIM)
    value_grad_low = value_acc.astype(jnp.bfloat16)
    query_full_grad = dot_first(normed_in, query_low)
    key_full_grad = dot_first(normed_in, key_low)
    value_full_grad = dot_first(normed_in, value_grad_low)
    normed_in_grad = sum_normed(
        dot_last(query_low, query_full)
        + dot_last(key_low, key_full)
        + dot_last(value_grad_low, value_full)
    )
    input_term, first_term = norm_backward(
        input_rows, inverse_in, first_gain, normed_in_grad, model_width
    )
    in_grad = grad_rows + input_term
    summed = (
        lax.psum_scatter(query_full_grad, "gx", scatter_dimension=0, tiled=True),
        lax.psum_scatter(key_full_grad, "gx", scatter_dimension=0, tiled=True),
        lax.psum_scatter(value_full_grad, "gx", scatter_dimension=0, tiled=True),
        lax.psum_scatter(out_full_grad, "gx", scatter_dimension=1, tiled=True),
        lax.psum_scatter(gate_full_grad, "gx", scatter_dimension=0, tiled=True),
        lax.psum_scatter(up_full_grad, "gx", scatter_dimension=0, tiled=True),
        lax.psum_scatter(down_full_grad, "gx", scatter_dimension=1, tiled=True),
    )
    gains = lax.psum((first_term, second_term), "gx")
    return (
        layer_out,
        in_grad,
        gains[0],
        summed[0],
        summed[1],
        summed[2],
        summed[3],
        gains[1],
        summed[4],
        summed[5],
        summed[6],
    )


def solution(mesh):
    placed = (
        P("gx", "gy"),
        P("gy"),
        P("gx", "gy"),
        P("gx", "gy"),
        P("gx", "gy"),
        P("gy", "gx"),
        P("gy"),
        P("gx", "gy"),
        P("gx", "gy"),
        P("gy", "gx"),
        P("gx", "gy"),
    )
    return jax.shard_map(
        shards,
        mesh=mesh,
        in_specs=placed,
        out_specs=(
            P("gx", "gy"),
            P("gx", "gy"),
            P("gy"),
            P("gx", "gy"),
            P("gx", "gy"),
            P("gx", "gy"),
            P("gy", "gx"),
            P("gy"),
            P("gx", "gy"),
            P("gx", "gy"),
            P("gy", "gx"),
        ),
        check_vma=False,
    )
```

profile of v0, /device:TPU:0, one launch (start us, length us, event | category | flops | bytes accessed | tf_op | source)
XLA Modules:
  0.0 1154.3 jit_solution(1140791852742636001)
XLA Ops:
  9.0 8.3 psum.42
  19.4 33.7 %all_gather.34 = bf16[1536,192]{1,0:T(8,128)(2,1)S(1)} all-gather(bf16[192,192]{1,0:T(8,128)(2,1)} %param.42), channel_id=1, replica_groups=mesh['gx'=8,'gy'=4] {'gx'}, dimensions={0}, use_global_device_ids=true | all-gather | bytes 663552 | tf_op jit(solution)/shard_map/all_gather | solution.py:179
  53.0 7.8 all_gather.33
  61.4 4.2 collective-permute-start.8
  66.9 4.5 collective-permute-start.4
  76.6 33.2 %all_gather.36 = bf16[1536,192]{1,0:T(8,128)(2,1)S(1)} all-gather(bf16[192,192]{1,0:T(8,128)(2,1)S(1)} %copy-done.63), channel_id=1, replica_groups=mesh['gx'=8,'gy'=4] {'gx'}, dimensions={0}, use_global_device_ids=true | all-gather | bytes 663552 | tf_op jit(solution)/shard_map/all_gather | solution.py:180
  119.3 4.0 collective-permute-start.1
  140.0 8.3 all_gather.42
  148.3 23.3 %reduce-scatter.34.cloned.1.call-done = bf16[384,256]{1,0:T(8,128)(2,1)} async-done(((bf16[1536,256]{1,0:T(8,128)(2,1)}), bf16[384,256]{1,0:T(8,128)(2,1)}) %reduce-scatter.34.cloned.1.call-update) | async-done | bytes 196624
  172.9 5.8 psum.43
  178.7 8.8 all_gather.38
  187.5 46.9 %all-gather.12.cloned.1.call-done = bf16[1536,1024]{1,0:T(8,128)(2,1)} async-done(((bf16[192,1024]{1,0:T(8,128)(2,1)}), bf16[1536,1024]{1,0:T(8,128)(2,1)}) %all-gather.12.cloned.1.call-update) | async-done | bytes 3145744 | tf_op jit(solution)/shard_map/all_gather | solution.py:185
  238.2 57.5 %all-gather.10.cloned.1.call-done = bf16[1536,1024]{1,0:T(8,128)(2,1)} async-done(((bf16[192,1024]{1,0:T(8,128)(2,1)}), bf16[1536,1024]{1,0:T(8,128)(2,1)}) %all-gather.10.cloned.1.call-update) | async-done | bytes 3145744 | tf_op jit(solution)/shard_map/all_gather | solution.py:184
  299.6 57.5 %all-gather.14.cloned.1.call-done = bf16[1024,1536]{0,1:T(8,128)(2,1)} async-done(((bf16[1024,192]{0,1:T(8,128)(2,1)}), bf16[1024,1536]{0,1:T(8,128)(2,1)}) %all-gather.14.cloned.1.call-update) | async-done | bytes 3145744 | tf_op jit(solution)/shard_map/all_gather | solution.py:186
  357.1 5.0 multiply_convert_fusion
  366.7 4.0 convolution_convert_fusion
  373.1 15.6 %reduce-scatter.38.cloned.1.call-done = bf16[384,256]{1,0:T(8,128)(2,1)} async-done(((bf16[1536,256]{1,0:T(8,128)(2,1)}), bf16[384,256]{1,0:T(8,128)(2,1)}) %reduce-scatter.38.cloned.1.call-update) | async-done | bytes 196624
  390.5 5.7 psum.44
  396.4 8.9 all_gather.43
  428.5 10.8 collective-permute-done.16
  440.6 4.6 collective-permute-done.17
  451.4 7.1 collective-permute-done.19
  467.3 7.3 collective-permute-done.24
  508.0 18.4 %all-reduce = (f32[384]{0:T(512)}, f32[384]{0:T(512)}) all-reduce(f32[384]{0:T(512)S(1)} %get-tuple-element.470, f32[384]{0:T(512)S(1)} %copy-done.96), channel_id=1, replica_groups=mesh['gx'=8,'gy'=4] {'gx'}, use_global_device_ids=true, to_apply=%region_57.58 | all-reduce | flops 768 | bytes 6144 | tf_op jit(solution)/shard_map/psum | solution.py:334
  526.4 6.0 psum.45
  533.5 38.0 %reduce-scatter.24.cloned.1.call-done = f32[192,192]{1,0:T(8,128)} async-done(((f32[1536,192]{1,0:T(8,128)}), f32[192,192]{1,0:T(8,128)}) %reduce-scatter.24.cloned.1.call-update) | async-done | bytes 147472 | tf_op jit(solution)/shard_map/reduce_scatter | solution.py:328
  571.6 68.2 %reduce-scatter.22.cloned.1.call-done = f32[192,192]{1,0:T(8,128)} async-done(((f32[1536,192]{1,0:T(8,128)}), f32[192,192]{1,0:T(8,128)}) %reduce-scatter.22.cloned.1.call-update) | async-done | bytes 147472 | tf_op jit(solution)/shard_map/reduce_scatter | solution.py:327
  639.7 72.0 %reduce-scatter.26.cloned.1.call-done = f32[384,192]{0,1:T(8,128)} async-done(((f32[384,1536]{0,1:T(8,128)}), f32[384,192]{0,1:T(8,128)}) %reduce-scatter.26.cloned.1.call-update) | async-done | bytes 294928 | tf_op jit(solution)/shard_map/reduce_scatter | solution.py:329
  711.8 72.2 %reduce-scatter.20.cloned.1.call-done = f32[192,384]{1,0:T(8,128)} async-done(((f32[1536,384]{1,0:T(8,128)}), f32[192,384]{1,0:T(8,128)}) %reduce-scatter.20.cloned.1.call-update) | async-done | bytes 294928 | tf_op jit(solution)/shard_map/reduce_scatter | solution.py:326
  783.9 121.0 %reduce-scatter.32.cloned.1.call-done = f32[1024,192]{0,1:T(8,128)} async-done(((f32[1024,1536]{0,1:T(8,128)}), f32[1024,192]{0,1:T(8,128)}) %reduce-scatter.32.cloned.1.call-update) | async-done | bytes 786448 | tf_op jit(solution)/shard_map/reduce_scatter | solution.py:332
  905.0 121.2 %reduce-scatter.30.cloned.1.call-done = f32[192,1024]{1,0:T(8,128)} async-done(((f32[1536,1024]{1,0:T(8,128)}), f32[192,1024]{1,0:T(8,128)}) %reduce-scatter.30.cloned.1.call-update) | async-done | bytes 786448 | tf_op jit(solution)/shard_map/reduce_scatter | solution.py:331
  1026.2 121.2 %reduce-scatter.28.cloned.1.call-done = f32[192,1024]{1,0:T(8,128)} async-done(((f32[1536,1024]{1,0:T(8,128)}), f32[192,1024]{1,0:T(8,128)}) %reduce-scatter.28.cloned.1.call-update) | async-done | bytes 786448 | tf_op jit(solution)/shard_map/reduce_scatter | solution.py:330
  (367 shorter events, 128.9 us)
Async XLA Ops:
  7.2 103.2 %all-gather.6.cloned.1.call-start = ((), (), s32[]{:S(2)}) async-start(), calls=%async_computation.11 | async-start | bytes 1327104 | tf_op jit(solution)/shard_map/all_gather | solution.py:178
  7.9 127.1 %all-gather.8.cloned.1.call-start = ((), (), s32[]{:S(2)}) async-start(), calls=%async_computation.12 | async-start | bytes 1327104 | tf_op jit(solution)/shard_map/all_gather | solution.py:181
  61.4 51.6 %collective-permute-start.8 = (bf16[256,192]{0,1:T(8,128)(2,1)S(1)}, bf16[256,192]{0,1:T(8,128)(2,1)S(1)}, u32[]{:S(2)}, u32[]{:S(2)}) collective-permute-start(bf16[256,192]{0,1:T(8,128)(2,1)S(1)} %bitcast.645), channel_id=1, source_target_pairs={{0,20},{4,24},{8,28},{1,21},{5,25},{9,29},{2,22},{6,26},{10,30},{3... | collective-permute-start | bytes 294920 | tf_op jit(solution)/shard_map/ppermute | solution.py:21
  65.6 48.7 %collective-permute-start.6 = (bf16[256,192]{0,1:T(8,128)(2,1)S(1)}, bf16[256,192]{0,1:T(8,128)(2,1)S(1)}, u32[]{:S(2)}, u32[]{:S(2)}) collective-permute-start(bf16[256,192]{0,1:T(8,128)(2,1)S(1)} %bitcast.646), channel_id=1, source_target_pairs={{0,16},{4,20},{8,24},{12,28},{1,17},{5,21},{9,25},{13,29},{2,18},{... | collective-permute-start | bytes 294920 | tf_op jit(solution)/shard_map/ppermute | solution.py:21
  66.9 50.6 %collective-permute-start.4 = (bf16[256,192]{0,1:T(8,128)(2,1)S(1)}, bf16[256,192]{0,1:T(8,128)(2,1)S(1)}, u32[]{:S(2)}, u32[]{:S(2)}) collective-permute-start(bf16[256,192]{0,1:T(8,128)(2,1)S(1)} %bitcast.647), channel_id=1, source_target_pairs={{0,12},{4,16},{8,20},{12,24},{16,28},{1,13},{5,17},{9,21},{13,25},... | collective-permute-start | bytes 294920 | tf_op jit(solution)/shard_map/ppermute | solution.py:21
  71.5 47.9 %collective-permute-start.2 = (bf16[256,192]{0,1:T(8,128)(2,1)S(1)}, bf16[256,192]{0,1:T(8,128)(2,1)S(1)}, u32[]{:S(2)}, u32[]{:S(2)}) collective-permute-start(bf16[256,192]{0,1:T(8,128)(2,1)S(1)} %bitcast.648), channel_id=1, source_target_pairs={{0,8},{4,12},{8,16},{12,20},{16,24},{20,28},{1,9},{5,13},{9,17},{1... | collective-permute-start | bytes 294920 | tf_op jit(solution)/shard_map/ppermute | solution.py:21
  72.8 50.9 %collective-permute-start = (bf16[256,192]{0,1:T(8,128)(2,1)S(1)}, bf16[256,192]{0,1:T(8,128)(2,1)}, u32[]{:S(2)}, u32[]{:S(2)}) collective-permute-start(bf16[256,192]{0,1:T(8,128)(2,1)S(1)} %bitcast.649), channel_id=1, source_target_pairs={{0,4},{4,8},{8,12},{12,16},{16,20},{20,24},{24,28},{1,5},{5,9},{9,... | collective-permute-start | bytes 294920 | tf_op jit(solution)/shard_map/ppermute | solution.py:21
  76.5 95.1 %reduce-scatter.34.cloned.1.call-start = ((), (), s32[]{:S(2)}) async-start(), calls=%async_computation.23 | async-start | bytes 983040
  138.2 96.2 %all-gather.12.cloned.1.call-start = ((), (), s32[]{:S(2)}) async-start(), calls=%async_computation.14 | async-start | bytes 3538944 | tf_op jit(solution)/shard_map/all_gather | solution.py:185
  138.8 156.9 %all-gather.10.cloned.1.call-start = ((), (), s32[]{:S(2)}) async-start(), calls=%async_computation.13 | async-start | bytes 3538944 | tf_op jit(solution)/shard_map/all_gather | solution.py:184
  139.4 217.7 %all-gather.14.cloned.1.call-start = ((), (), s32[]{:S(2)}) async-start(), calls=%async_computation.15 | async-start | bytes 3538944 | tf_op jit(solution)/shard_map/all_gather | solution.py:186
  140.0 248.7 %reduce-scatter.38.cloned.1.call-start = ((), (), s32[]{:S(2)}) async-start(), calls=%async_computation.25 | async-start | bytes 983040
  366.6 138.8 %reduce-scatter.36.cloned.1.call-start = ((), (), s32[]{:S(2)}) async-start(), calls=%async_computation.24 | async-start | bytes 983040
  373.0 133.6 %reduce-scatter.40.cloned.1.call-start = ((), (), s32[]{:S(2)}) async-start(), calls=%async_computation.26 | async-start | bytes 983040
  409.3 15.5 %collective-permute-start.14 = (bf16[256,192]{0,1:T(8,128)(2,1)}, bf16[256,192]{0,1:T(8,128)(2,1)}, u32[]{:S(2)}, u32[]{:S(2)}) collective-permute-start(bf16[256,192]{0,1:T(8,128)(2,1)} %get-tuple-element.389), channel_id=1, source_target_pairs={{4,0},{8,4},{12,8},{16,12},{20,16},{24,20},{28,24},{5,1},{9,5},{13... | collective-permute-start | bytes 294920 | tf_op jit(solution)/shard_map/ppermute | solution.py:21
  420.8 18.5 %collective-permute-start.16 = (bf16[256,192]{0,1:T(8,128)(2,1)S(1)}, bf16[256,192]{0,1:T(8,128)(2,1)S(1)}, u32[]{:S(2)}, u32[]{:S(2)}) collective-permute-start(bf16[256,192]{0,1:T(8,128)(2,1)S(1)} %copy-done.71), channel_id=1, source_target_pairs={{12,0},{16,4},{20,8},{24,12},{28,16},{13,1},{17,5},{21,9},{25,13},... | collective-permute-start | bytes 294920 | tf_op jit(solution)/shard_map/ppermute | solution.py:21
  422.2 23.0 %collective-permute-start.17 = (bf16[256,192]{0,1:T(8,128)(2,1)S(1)}, bf16[256,192]{0,1:T(8,128)(2,1)S(1)}, u32[]{:S(2)}, u32[]{:S(2)}) collective-permute-start(bf16[256,192]{0,1:T(8,128)(2,1)S(1)} %copy-done.75), channel_id=1, source_target_pairs={{16,0},{20,4},{24,8},{28,12},{17,1},{21,5},{25,9},{29,13},{18,2},{... | collective-permute-start | bytes 294920 | tf_op jit(solution)/shard_map/ppermute | solution.py:21
  423.5 26.6 %collective-permute-start.18 = (bf16[256,192]{0,1:T(8,128)(2,1)S(1)}, bf16[256,192]{0,1:T(8,128)(2,1)S(1)}, u32[]{:S(2)}, u32[]{:S(2)}) collective-permute-start(bf16[256,192]{0,1:T(8,128)(2,1)S(1)} %copy-done.79), channel_id=1, source_target_pairs={{20,0},{24,4},{28,8},{21,1},{25,5},{29,9},{22,2},{26,6},{30,10},{2... | collective-permute-start | bytes 294920 | tf_op jit(solution)/shard_map/ppermute | solution.py:21
  424.9 33.7 %collective-permute-start.19 = (bf16[256,192]{0,1:T(8,128)(2,1)S(1)}, bf16[256,192]{0,1:T(8,128)(2,1)S(1)}, u32[]{:S(2)}, u32[]{:S(2)}) collective-permute-start(bf16[256,192]{0,1:T(8,128)(2,1)S(1)} %copy-done.83), channel_id=1, source_target_pairs={{24,0},{28,4},{25,1},{29,5},{26,2},{30,6},{27,3},{31,7}} | collective-permute-start | bytes 294920 | tf_op jit(solution)/shard_map/ppermute | solution.py:21
  426.8 35.5 %collective-permute-start.20 = (bf16[256,192]{0,1:T(8,128)(2,1)S(1)}, bf16[256,192]{0,1:T(8,128)(2,1)S(1)}, u32[]{:S(2)}, u32[]{:S(2)}) collective-permute-start(bf16[256,192]{0,1:T(8,128)(2,1)S(1)} %copy-done.87), channel_id=1, source_target_pairs={{28,0},{29,1},{30,2},{31,3}} | collective-permute-start | bytes 294920 | tf_op jit(solution)/shard_map/ppermute | solution.py:21
  439.3 25.3 %collective-permute-start.21 = (bf16[256,192]{0,1:T(8,128)(2,1)S(1)}, bf16[256,192]{0,1:T(8,128)(2,1)S(1)}, u32[]{:S(2)}, u32[]{:S(2)}) collective-permute-start(bf16[256,192]{0,1:T(8,128)(2,1)S(1)} %copy-done.65), channel_id=1, source_target_pairs={{4,0},{8,4},{12,8},{16,12},{20,16},{24,20},{28,24},{5,1},{9,5},{13... | collective-permute-start | bytes 294920 | tf_op jit(solution)/shard_map/ppermute | solution.py:21
  445.2 20.7 %collective-permute-start.22 = (bf16[256,192]{0,1:T(8,128)(2,1)S(1)}, bf16[256,192]{0,1:T(8,128)(2,1)S(1)}, u32[]{:S(2)}, u32[]{:S(2)}) collective-permute-start(bf16[256,192]{0,1:T(8,128)(2,1)S(1)} %copy-done.67), channel_id=1, source_target_pairs={{8,0},{12,4},{16,8},{20,12},{24,16},{28,20},{9,1},{13,5},{17,9},{2... | collective-permute-start | bytes 294920 | tf_op jit(solution)/shard_map/ppermute | solution.py:21
  450.1 17.2 %collective-permute-start.23 = (bf16[256,192]{0,1:T(8,128)(2,1)S(1)}, bf16[256,192]{0,1:T(8,128)(2,1)S(1)}, u32[]{:S(2)}, u32[]{:S(2)}) collective-permute-start(bf16[256,192]{0,1:T(8,128)(2,1)S(1)} %copy-done.69), channel_id=1, source_target_pairs={{12,0},{16,4},{20,8},{24,12},{28,16},{13,1},{17,5},{21,9},{25,13},... | collective-permute-start | bytes 294920 | tf_op jit(solution)/shard_map/ppermute | solution.py:21
  458.5 16.1 %collective-permute-start.24 = (bf16[256,192]{0,1:T(8,128)(2,1)S(1)}, bf16[256,192]{0,1:T(8,128)(2,1)S(1)}, u32[]{:S(2)}, u32[]{:S(2)}) collective-permute-start(bf16[256,192]{0,1:T(8,128)(2,1)S(1)} %copy-done.73), channel_id=1, source_target_pairs={{16,0},{20,4},{24,8},{28,12},{17,1},{21,5},{25,9},{29,13},{18,2},{... | collective-permute-start | bytes 294920 | tf_op jit(solution)/shard_map/ppermute | solution.py:21
  462.2 16.0 %collective-permute-start.25 = (bf16[256,192]{0,1:T(8,128)(2,1)S(1)}, bf16[256,192]{0,1:T(8,128)(2,1)S(1)}, u32[]{:S(2)}, u32[]{:S(2)}) collective-permute-start(bf16[256,192]{0,1:T(8,128)(2,1)S(1)} %copy-done.77), channel_id=1, source_target_pairs={{20,0},{24,4},{28,8},{21,1},{25,5},{29,9},{22,2},{26,6},{30,10},{2... | collective-permute-start | bytes 294920 | tf_op jit(solution)/shard_map/ppermute | solution.py:21
  483.1 88.4 %reduce-scatter.24.cloned.1.call-start = ((), (), s32[]{:S(2)}) async-start(), calls=%async_computation.18 | async-start | bytes 1769472 | tf_op jit(solution)/shard_map/reduce_scatter | solution.py:328
  484.8 154.9 %reduce-scatter.22.cloned.1.call-start = ((), (), s32[]{:S(2)}) async-start(), calls=%async_computation.17 | async-start | bytes 1769472 | tf_op jit(solution)/shard_map/reduce_scatter | solution.py:327
  486.5 225.3 %reduce-scatter.26.cloned.1.call-start = ((), (), s32[]{:S(2)}) async-start(), calls=%async_computation.19 | async-start | bytes 2654208 | tf_op jit(solution)/shard_map/reduce_scatter | solution.py:329
  488.7 295.3 %reduce-scatter.20.cloned.1.call-start = ((), (), s32[]{:S(2)}) async-start(), calls=%async_computation.16 | async-start | bytes 2654208 | tf_op jit(solution)/shard_map/reduce_scatter | solution.py:326
  490.8 414.2 %reduce-scatter.32.cloned.1.call-start = ((), (), s32[]{:S(2)}) async-start(), calls=%async_computation.22 | async-start | bytes 7077888 | tf_op jit(solution)/shard_map/reduce_scatter | solution.py:332
  495.7 530.5 %reduce-scatter.30.cloned.1.call-start = ((), (), s32[]{:S(2)}) async-start(), calls=%async_computation.21 | async-start | bytes 7077888 | tf_op jit(solution)/shard_map/reduce_scatter | solution.py:331
  500.6 646.7 %reduce-scatter.28.cloned.1.call-start = ((), (), s32[]{:S(2)}) async-start(), calls=%async_computation.20 | async-start | bytes 7077888 | tf_op jit(solution)/shard_map/reduce_scatter | solution.py:330
  (102 other events, 1381.1 us)
Sparse Core Ops, SparseCore 0:
  10.2 47.3 all-gather.5
  76.7 41.9 all-gather.7
  138.3 33.2 reduce-scatter.33
  173.9 60.4 all-gather.11
  236.6 59.0 all-gather.9
  298.0 59.0 all-gather.13
  366.7 21.8 reduce-scatter.37
  391.2 23.2 reduce-scatter.35
  483.3 19.5 reduce-scatter.39
  506.7 64.8 reduce-scatter.23
  576.0 63.7 reduce-scatter.21
  643.7 68.0 reduce-scatter.25
  715.8 68.0 reduce-scatter.19
  788.0 116.9 reduce-scatter.31
  909.0 117.1 reduce-scatter.29
  1030.2 117.1 reduce-scatter.27
where the time goes:
time: 1160 us; the launch traced here: 1150 us
  waiting for transfers between devices  859 us (74%)
  blocking collectives  145 us (12%)
  starting transfers between devices  54.1 us (5%)
  matrix products  47.5 us (4%)
  local copies, waits for them, and re-layouts  23.6 us (2%)
  between operations  16 us (1%)
    reduce_scatter x1, waiting for transfers between devices, shards(): lax.psum_scatter(gate_full_grad, 'gx', scatter_dimension=0, tiled=True)  121 us
    reduce_scatter x1, waiting for transfers between devices, shards(): lax.psum_scatter(up_full_grad, 'gx', scatter_dimension=0, tiled=True)  121 us
    reduce_scatter x1, waiting for transfers between devices, shards(): lax.psum_scatter(down_full_grad, 'gx', scatter_dimension=1, tiled=True)  121 us
    reduce_scatter x1, waiting for transfers between devices, shards(): lax.psum_scatter(query_full_grad, 'gx', scatter_dimension=0, tiled=True)  72.2 us
    reduce_scatter x1, waiting for transfers between devices, shards(): lax.psum_scatter(out_full_grad, 'gx', scatter_dimension=1, tiled=True)  72 us
    reduce_scatter x1, waiting for transfers between devices, shards(): lax.psum_scatter(key_full_grad, 'gx', scatter_dimension=0, tiled=True)  68.2 us
    all_gather x1, waiting for transfers between devices, shards(): lax.all_gather(down_weight, 'gx', axis=1, tiled=True)  57.5 us
    all_gather x1, waiting for transfers between devices, shards(): lax.all_gather(gate_weight, 'gx', axis=0, tiled=True)  57.5 us
  transfers between devices with their start and end apart: 44, of which 21 were waited for; matrix products, arithmetic and copies ran while one was open for 5% of the time, Pallas kernels for 0%

commit v1 on v0

v1 whole, which is shorter than its diff:
```python
import jax
import jax.numpy as jnp
from jax import lax
from jax.experimental import pallas as pl
from jax.experimental.pallas import tpu as pltpu
from jax.sharding import PartitionSpec as P

HEAD_DIM = 96
PROMPT_DEV = 4
CONT_DEV = 4
LINE_MAX = 8

eps = 1e-05
neg_big = -1e30
rope_base = 100000.0
f32 = jnp.float32
bf16 = jnp.bfloat16


def dims(left, right, left_axis, right_axis):
    return lax.dot_general(
        left, right, (((left_axis,), (right_axis,)), ((), ())), preferred_element_type=f32
    )


class Place:
    def __init__(self):
        self.nx = lax.axis_size("gx")
        self.ny = lax.axis_size("gy")
        assert self.ny == 4 and self.nx % (PROMPT_DEV + CONT_DEV) == 0
        self.n = self.nx // 2
        gx = lax.axis_index("gx")
        gy = lax.axis_index("gy")
        self.z, self.y = gx // 2, gx % 2
        self.x, self.c = gy // 2, gy % 2
        self.gx, self.gy = gx, gy

    def swap_y(self, value):
        return lax.ppermute(value, "gx", [(i, i ^ 1) for i in range(self.nx)])

    def swap_gx(self, value, bit):
        return lax.ppermute(value, "gx", [(i, i ^ bit) for i in range(self.nx)])

    def swap_x(self, value):
        return lax.ppermute(value, "gy", [(i, i ^ 2) for i in range(self.ny)])

    def swap_c(self, value):
        return lax.ppermute(value, "gy", [(i, i ^ 1) for i in range(self.ny)])

    def shift(self, value, sources, step):
        pairs = [(2 * s + y, 2 * (s + step) + y) for s in sources for y in range(2)]
        return lax.ppermute(value, "gx", pairs)


def pair(flag, mine, other):
    return jnp.where(flag == 0, mine, other), jnp.where(flag == 0, other, mine)


def groups_by_y(place):
    return [[2 * z + y for z in range(place.n)] for y in range(2)]


def gather_line(place, piece):
    n, z = place.n, place.z
    if n > LINE_MAX:
        return lax.all_gather(piece, "gx", axis_index_groups=groups_by_y(place))
    ups, downs = {}, {}
    up = down = piece
    for k in range(1, n):
        up = place.shift(up, range(k - 1, n - 1), 1)
        down = place.shift(down, range(1, n - k + 1), -1)
        ups[k], downs[k] = up, down
    whole = jnp.zeros((n,) + piece.shape, piece.dtype)
    whole = lax.dynamic_update_index_in_dim(whole, piece, z, 0)
    for k in range(1, n):
        taken = jnp.where(z >= k, ups[k], downs[n - k])
        whole = lax.dynamic_update_index_in_dim(whole, taken, (z - k) % n, 0)
    return whole


def scatter_line(place, parts):
    n, z = place.n, place.z
    if n > LINE_MAX:
        return lax.psum_scatter(
            parts.astype(bf16), "gx", axis_index_groups=groups_by_y(place)
        ).astype(f32)

    def part(index):
        chosen = lax.dynamic_index_in_dim(parts, jnp.clip(index, 0, n - 1), 0, keepdims=False)
        return chosen.astype(f32)

    down = up = None
    for k in range(n - 1, 0, -1):
        send_down, send_up = part(z - k), part(z + k)
        if down is not None:
            send_down, send_up = send_down + down, send_up + up
        down = place.shift(send_down.astype(bf16), range(k, n), -1).astype(f32)
        up = place.shift(send_up.astype(bf16), range(0, n - k), 1).astype(f32)
    return part(z) + down + up


def split_y(place, rows_of_y):
    half = rows_of_y.shape[1] // 2
    low, high = rows_of_y[:, :half], rows_of_y[:, half:]
    mine = jnp.where(place.y == 0, low, high)
    other = jnp.where(place.y == 0, high, low)
    return mine, other


def join_y(place, summed):
    rows = summed.shape[0] // 2
    low, high = summed[:rows], summed[rows:]
    mine = jnp.where(place.y == 0, low, high)
    other = jnp.where(place.y == 0, high, low)
    return mine, place.swap_y(other.astype(bf16)).astype(f32)


def reduce_core(place, partial_rows):
    width = partial_rows.shape[1] // 4
    blocks = [partial_rows[:, i * width : (i + 1) * width] for i in range(4)]
    keep = [jnp.where(place.c == 0, blocks[2 * i], blocks[2 * i + 1]) for i in range(2)]
    send = [jnp.where(place.c == 0, blocks[2 * i + 1], blocks[2 * i]) for i in range(2)]
    got = place.swap_c(jnp.stack([s.astype(bf16) for s in send]))
    return [keep[i] + got[i].astype(f32) for i in range(2)]


def all_sum(place, partial_rows):
    first, second = reduce_core(place, partial_rows)
    first_got = place.swap_x(first.astype(bf16))
    second_got = place.swap_y(second.astype(bf16))
    first, second = first + first_got.astype(f32), second + second_got.astype(f32)
    first_got = place.swap_y(first.astype(bf16))
    second_got = place.swap_x(second.astype(bf16))
    first, second = first + first_got.astype(f32), second + second_got.astype(f32)
    both = jnp.stack([first.astype(bf16), second.astype(bf16)])
    other = place.swap_c(both)
    low, high = pair(place.c, both, other)
    whole = jnp.concatenate([low[0], high[0], low[1], high[1]], axis=1)
    return whole, own_rows(place, jnp.where(place.x == 0, first, second))


def own_rows(place, rows):
    half = rows.shape[0] // 2
    return jnp.where(place.y == 0, rows[:half], rows[half:])


def own_sum(place, partial_rows):
    first, second = reduce_core(place, partial_rows)
    mine = jnp.where(place.x == 0, first, second)
    other = jnp.where(place.x == 0, second, first)
    mine = mine + place.swap_x(other.astype(bf16)).astype(f32)
    half = mine.shape[0] // 2
    low, high = mine[:half], mine[half:]
    other = jnp.where(place.y == 0, high, low)
    return jnp.where(place.y == 0, low, high) + place.swap_y(other.astype(bf16)).astype(f32)


def spread(place, blocks):
    count, rows, cols = blocks.shape
    by_x = jnp.stack(pair(place.x, blocks, place.swap_x(blocks)))
    by_y = jnp.stack(pair(place.y, by_x, place.swap_y(by_x)))
    by_c = jnp.stack(pair(place.c, by_y, place.swap_c(by_y)))
    return jnp.transpose(by_c, (3, 1, 4, 2, 0, 5)).reshape(count, 2 * rows, 4 * cols)


def rope_tables(positions, half):
    freq = rope_base ** (-(2.0 * jnp.arange(half, dtype=f32)) / (2.0 * half))
    angle = freq[:, None] * positions.astype(f32)[None, :]
    return (jnp.cos(angle), jnp.sin(angle))


def rotate(values, cosine, sine):
    half = values.shape[1] // 2
    first, second = values[:, :half], values[:, half:]
    return jnp.concatenate(
        [first * cosine - second * sine, second * cosine + first * sine], axis=1
    )


def attend_kernel(count_ref, q_ref, own_ref, far_ref, out_ref, log_ref, *, block, scale):
    head = HEAD_DIM
    far = far_ref[...]
    key_far, value_far = far[:head].T, far[head:]
    key_own = own_ref[:head].T
    total = far.shape[1]
    for part in range(q_ref.shape[2] // block):
        cols = slice(part * block, (part + 1) * block)
        key_near, value_near = key_own[cols], own_ref[head:, cols]
        row = lax.broadcasted_iota(jnp.int32, (total, block), 0)
        seen = row < count_ref[part] * block
        near_row = lax.broadcasted_iota(jnp.int32, (block, block), 0)
        near_col = lax.broadcasted_iota(jnp.int32, (block, block), 1)
        causal = near_row <= near_col
        for h in range(q_ref.shape[0]):
            query = q_ref[h, :, cols]
            score_far = jnp.where(seen, dims(key_far, query, 1, 0) * scale, neg_big)
            score_near = jnp.where(causal, dims(key_near, query, 1, 0) * scale, neg_big)
            top = jnp.maximum(
                jnp.max(score_far, axis=0, keepdims=True), jnp.max(score_near, axis=0, keepdims=True)
            )
            weight_far = jnp.exp(score_far - top)
            weight_near = jnp.exp(score_near - top)
            total_weight = jnp.sum(weight_far, axis=0, keepdims=True) + jnp.sum(
                weight_near, axis=0, keepdims=True
            )
            out = dims(value_far, weight_far.astype(bf16), 1, 0) + dims(
                value_near, weight_near.astype(bf16), 1, 0
            )
            out_ref[h, :, cols] = out / total_weight
            log_ref[h, :, cols] = top + jnp.log(total_weight)


def attend_back_kernel(
    count_ref,
    q_ref,
    own_ref,
    far_ref,
    grad_ref,
    out_ref,
    log_ref,
    dq_ref,
    down_ref,
    dfar_ref,
    *,
    block,
    scale,
):
    head = HEAD_DIM
    far = far_ref[...]
    key_far_t, value_far_t = far[:head], far[head:]
    key_far, value_far = key_far_t.T, value_far_t.T
    key_own, value_own = own_ref[:head].T, own_ref[head:].T
    total = far.shape[1]
    for part in range(q_ref.shape[2] // block):
        cols = slice(part * block, (part + 1) * block)
        key_near, value_near = key_own[cols], value_own[cols]
        key_near_t = own_ref[:head, cols]
        row = lax.broadcasted_iota(jnp.int32, (total, block), 0)
        seen = row < count_ref[part] * block
        near_row = lax.broadcasted_iota(jnp.int32, (block, block), 0)
        near_col = lax.broadcasted_iota(jnp.int32, (block, block), 1)
        causal = near_row <= near_col
        dk_near = jnp.zeros((head, block), f32)
        dv_near = jnp.zeros((head, block), f32)
        for h in range(q_ref.shape[0]):
            query, grad = q_ref[h, :, cols], grad_ref[h, :, cols]
            delta = jnp.sum(grad.astype(f32) * out_ref[h, :, cols], axis=0, keepdims=True)
            log_total = log_ref[h, :, cols]

            def one(key, value, allowed):
                score = dims(key, query, 1, 0) * scale
                prob = jnp.where(allowed, jnp.exp(score - log_total), 0.0)
                change = (prob * (dims(value, grad, 1, 0) - delta)).astype(bf16)
                return prob.astype(bf16), change

            prob_far, change_far = one(key_far, value_far, seen)
            prob_near, change_near = one(key_near, value_near, causal)
            dq_ref[h, :, cols] = (
                dims(key_far_t, change_far, 1, 0) + dims(key_near_t, change_near, 1, 0)
            ) * scale
            dk_far = dims(query, change_far, 1, 1) * scale
            dv_far = dims(grad, prob_far, 1, 1)
            if part == 0 and h == 0:
                dfar_ref[:head] = dk_far
                dfar_ref[head:] = dv_far
            else:
                dfar_ref[:head] += dk_far
                dfar_ref[head:] += dv_far
            dk_near += dims(query, change_near, 1, 1) * scale
            dv_near += dims(grad, prob_near, 1, 1)
        down_ref[:head, cols] = dk_near
        down_ref[head:, cols] = dv_near


def on_core(kernel, out_shape, count, *operands):
    whole = pl.BlockSpec(memory_space=pltpu.VMEM)
    return pl.pallas_call(
        kernel,
        out_shape=out_shape,
        in_specs=[pl.BlockSpec(memory_space=pltpu.SMEM)] + [whole] * len(operands),
        out_specs=jax.tree.map(lambda s: whole, out_shape),
    )(count, *operands)


def shards(
    layer_in,
    first_gain,
    query_weight,
    key_matrix,
    value_matrix,
    out_weight,
    second_gain,
    gate_weight,
    up_weight,
    down_weight,
    out_grad,
):
    place = Place()
    n, z, y = place.n, place.z, place.y
    block = layer_in.shape[0]
    tokens = 2 * block
    width = layer_in.shape[1]
    model_width = width * place.ny
    scale = HEAD_DIM ** (-0.5)
    group = (PROMPT_DEV + CONT_DEV) // 2
    prompts = PROMPT_DEV // 2
    z_in = z % group

    def halves(*matrices):
        mine, other = zip(*(split_y(place, m) for m in matrices))
        return jnp.concatenate(mine, axis=1), jnp.concatenate(other, axis=1)

    def rows_of_z(mine, got):
        low, high = pair(y, mine, got)
        return jnp.concatenate([low, high], axis=0)

    qkv_mine, qkv_other = halves(query_weight, key_matrix, value_matrix)
    out_mine, out_other = halves(out_weight.T)
    gu_mine, gu_other = halves(gate_weight, up_weight)
    down_mine, down_other = halves(down_weight.T)
    qkv_full = gather_line(place, rows_of_z(qkv_mine, place.swap_y(qkv_other)))
    out_full = gather_line(place, rows_of_z(out_mine, place.swap_y(out_other)))
    gu_full = gather_line(place, rows_of_z(gu_mine, place.swap_y(gu_other)))
    down_full = gather_line(place, rows_of_z(down_mine, place.swap_y(down_other)))
    qkv_full = qkv_full.reshape(model_width, -1)
    out_full = out_full.reshape(model_width, -1)
    gu_full = gu_full.reshape(model_width, -1)
    down_full = down_full.reshape(model_width, -1)
    hidden_dev = down_full.shape[1]
    heads = out_full.shape[1] // HEAD_DIM

    both = spread(place, jnp.stack([layer_in, out_grad]))
    rows_in, grad_low = both[0].astype(f32), both[1]
    gains = jnp.stack([first_gain, second_gain])
    gains = jnp.stack(pair(place.x, gains, place.swap_x(gains)))
    gains = jnp.stack(pair(place.c, gains, place.swap_c(gains)))
    gains = jnp.transpose(gains, (2, 1, 0, 3)).reshape(2, 1, model_width)

    inverse_in = lax.rsqrt(jnp.mean(rows_in * rows_in, axis=1, keepdims=True) + eps)
    normed_in = (rows_in * inverse_in * gains[0]).astype(bf16)

    qkv = dims(qkv_full, normed_in, 0, 1).reshape(-1, HEAD_DIM, tokens)
    offset = 2 * z_in + jnp.arange(2, dtype=jnp.int32)
    within = jnp.arange(block, dtype=jnp.int32)
    positions = (jnp.minimum(offset, PROMPT_DEV)[:, None] * block + within[None, :]).reshape(-1)
    cosine, sine = rope_tables(positions, HEAD_DIM // 2)
    turned = rotate(qkv[: heads + 1], cosine, sine).astype(bf16)
    query = turned[:heads]
    own = jnp.concatenate([turned[heads], qkv[heads + 1].astype(bf16)], axis=0)
    slots = [own] * prompts
    moving = own
    for k in range(1, group):
        sources = [
            s for s in range(n) if 0 <= s % group - (k - 1) < prompts and s % group + 1 < group
        ]
        moving = place.shift(moving, sources, 1)
        slots = [jnp.where(z_in == i + k, moving, slots[i]) for i in range(prompts)]
    far = jnp.concatenate(slots, axis=1)
    count = jnp.minimum(offset, PROMPT_DEV)

    def kernel(body):
        return lambda *refs: body(*refs, block=block, scale=scale)

    attended, log_total = on_core(
        kernel(attend_kernel),
        (
            jax.ShapeDtypeStruct((heads, HEAD_DIM, tokens), f32),
            jax.ShapeDtypeStruct((heads, 1, tokens), f32),
        ),
        count,
        query,
        own,
        far,
    )
    attended_low = attended.astype(bf16).reshape(heads * HEAD_DIM, tokens)
    branch, branch_own = all_sum(place, dims(attended_low, out_full, 0, 1))

    hidden = rows_in + branch.astype(f32)
    hidden_own = layer_in.astype(f32) + branch_own
    inverse_mid = lax.rsqrt(jnp.mean(hidden * hidden, axis=1, keepdims=True) + eps)
    normed_mid = (hidden * inverse_mid * gains[1]).astype(bf16)
    gate_up = dims(normed_mid, gu_full, 1, 0)
    gate, up = gate_up[:, :hidden_dev], gate_up[:, hidden_dev:]
    sigmoid = jax.nn.sigmoid(gate)
    active = (gate * sigmoid * up).astype(bf16)
    layer_out = (hidden_own + own_sum(place, dims(active, down_full, 1, 1))).astype(bf16)

    def scattered(parts):
        parts = parts.astype(bf16).reshape(n, model_width // n, -1)
        return join_y(place, scatter_line(place, parts))

    down_grad = scattered(dims(grad_low, active, 0, 0))
    active_grad = dims(grad_low, down_full, 1, 0)
    gate_low = (active_grad * up * sigmoid * (1.0 + gate * (1.0 - sigmoid))).astype(bf16)
    up_low = (active_grad * gate * sigmoid).astype(bf16)
    gu_low = jnp.concatenate([gate_low, up_low], axis=1)
    gu_grad = scattered(dims(normed_mid, gu_low, 0, 0))
    mid_grad, mid_grad_own = all_sum(place, dims(gu_low, gu_full, 1, 1))

    def norm_back(rows, inverse, gain, grad):
        scaled = grad * gain
        inner = jnp.sum(scaled * rows, axis=1, keepdims=True)
        return scaled, inverse**3 * inner / model_width

    mid_grad = mid_grad.astype(f32)
    scaled, pull = norm_back(hidden, inverse_mid, gains[1], mid_grad)
    through = (grad_low.astype(f32) + inverse_mid * scaled - hidden * pull).astype(bf16)
    inverse_own, pull_own = own_rows(place, inverse_mid), own_rows(place, pull)
    through_own = (
        out_grad.astype(f32)
        + inverse_own * mid_grad_own * second_gain[None, :]
        - hidden_own * pull_own
    )
    second_term = jnp.sum(mid_grad_own * hidden_own * inverse_own, axis=0)

    out_parts = dims(through, attended_low, 0, 1)
    branch_grad = dims(out_full, through, 0, 1).astype(bf16).reshape(heads, HEAD_DIM, tokens)
    query_back, own_back, far_back = on_core(
        kernel(attend_back_kernel),
        (
            jax.ShapeDtypeStruct((heads, HEAD_DIM, tokens), f32),
            jax.ShapeDtypeStruct(own.shape, f32),
            jax.ShapeDtypeStruct(far.shape, f32),
        ),
        count,
        query,
        own,
        far,
        branch_grad,
        attended,
        log_total,
    )
    query_low = rotate(query_back, cosine, -sine).astype(bf16).reshape(heads * HEAD_DIM, tokens)
    query_out = scattered(
        jnp.concatenate([dims(normed_in, query_low, 0, 1), out_parts], axis=1)
    )
    slots_back = [far_back[:, i * tokens : (i + 1) * tokens] for i in range(prompts)]
    for i in range(prompts):
        own_back = own_back + jnp.where(z_in == i, slots_back[i], 0.0)
    moving = None
    for k in range(group - 1, 0, -1):
        sources = [s for s in range(n) if 0 <= s % group - k < prompts]
        send = slots_back[0]
        for i in range(1, prompts):
            send = jnp.where(z_in - k == i, slots_back[i], send)
        if moving is not None:
            send = send + moving
        moving = place.shift(send.astype(bf16), sources, -1).astype(f32)
    own_back = own_back + moving
    key_low = rotate(own_back[None, :HEAD_DIM], cosine, -sine)[0].astype(bf16)
    key_value_low = jnp.concatenate([key_low, own_back[HEAD_DIM:].astype(bf16)], axis=0)
    key_value = scattered(dims(normed_in, key_value_low, 0, 1))
    qkv_low = jnp.concatenate([query_low, key_value_low], axis=0)
    first_own = own_sum(place, dims(qkv_low, qkv_full, 0, 1))
    input_own = layer_in.astype(f32)
    inverse_own = own_rows(place, inverse_in)
    scaled = first_own * first_gain[None, :]
    inner = jnp.sum(scaled * input_own, axis=1, keepdims=True)
    inner = inner + place.swap_c(inner)
    inner = inner + place.swap_x(inner)
    in_grad = (
        through_own + inverse_own * scaled - input_own * (inverse_own**3 * inner / model_width)
    )
    first_term = jnp.sum(first_own * input_own * inverse_own, axis=0)
    terms = jnp.stack([first_term, second_term])
    bit = 1
    while bit < place.nx:
        terms = terms + place.swap_gx(terms, bit)
        bit *= 2

    def columns(summed, start, stop):
        low, high = pair(y, summed[0][:, start:stop], summed[1][:, start:stop])
        return jnp.concatenate([low, high], axis=1)

    query_cols = heads * HEAD_DIM
    return (
        layer_out,
        in_grad,
        terms[0],
        columns(query_out, 0, query_cols),
        columns(key_value, 0, HEAD_DIM),
        columns(key_value, HEAD_DIM, 2 * HEAD_DIM),
        columns(query_out, query_cols, 2 * query_cols).T,
        terms[1],
        columns(gu_grad, 0, hidden_dev),
        columns(gu_grad, hidden_dev, 2 * hidden_dev),
        columns(down_grad, 0, hidden_dev).T,
    )


def solution(mesh):
    rows, cols, gain = P("gx", "gy"), P("gy", "gx"), P("gy")
    return jax.shard_map(
        shards,
        mesh=mesh,
        in_specs=(rows, gain, rows, rows, rows, cols, gain, rows, rows, cols, rows),
        out_specs=(rows, rows, gain, rows, rows, rows, cols, gain, rows, rows, cols),
        check_vma=False,
    )
```

time: 1160 us -> 547 us (0.47)
  waiting for transfers between devices: 859 us -> 96 us
  blocking collectives: 145 us -> 0 us
  starting transfers between devices: 54.1 us -> 199 us
  local copies, waits for them, and re-layouts: 23.6 us -> 110 us
  other arithmetic: 9.23 us -> 95.5 us
  matrix products: 47.5 us -> 21.3 us
  between operations: 16 us -> 3.52 us
  Pallas kernels: 0 us -> 11.9 us
    reduce_scatter x7 -> x0, waiting for transfers between devices: 614 us -> none  [the longest x1 121 us: shards(): lax.psum_scatter(gate_full_grad, 'gx', scatter_dimension=0, tiled=True)]
    all_gather x5 -> x0, waiting for transfers between devices: 162 us -> none  [the longest x1 57.5 us: shards(): lax.all_gather(down_weight, 'gx', axis=1, tiled=True)]
    ppermute x28 -> x90, starting transfers between devices: 53.2 us -> 199 us  [the longest x54 163 us: shift(): return lax.ppermute(value, 'gx', pairs)]
    all_gather x6 -> x0, blocking collectives: 101 us -> none  [the longest x1 33.7 us: shards(): lax.all_gather(key_matrix, 'gx', axis=0, tiled=True)]
    ppermute x28 -> x90, waiting for transfers between devices: 41.6 us -> 96 us  [the longest x54 55.2 us: shift(): return lax.ppermute(value, 'gx', pairs)]
    psum x5 -> x0, blocking collectives: 44.3 us -> none  [the longest x1 18.4 us: shards(): gains = lax.psum((first_term, second_term), 'gx')]
    unnamed x20 -> x0, waiting for transfers between devices: 41.3 us -> none
    convert_element_type x1 -> x10, local copies, waits for them, and re-layouts: 0.15 us -> 39.8 us  [the longest x2 11.5 us: shards(): rows_in, grad_low = (both[0].astype(f32), both[1])]
  transfers between devices with their start and end apart: 44 -> 90, of which waited for: 21 -> 23; matrix products, arithmetic and copies ran while one was open for 5% -> 35% of each run, Pallas kernels for 0% -> 2%
where the time goes in v1:
time: 547 us; the launch traced here: 537 us
  starting transfers between devices  199 us (36%)
  local copies, waits for them, and re-layouts  110 us (20%)
  waiting for transfers between devices  96 us (18%)
  other arithmetic  95.5 us (17%)
  matrix products  21.3 us (4%)
  Pallas kernels  11.9 us (2%)
    ppermute x54, starting transfers between devices, shift(): return lax.ppermute(value, 'gx', pairs)  163 us
    ppermute x54, waiting for transfers between devices, shift(): return lax.ppermute(value, 'gx', pairs)  55.2 us
    dynamic_update_slice x6, local copies, waits for them, and re-layouts, gather_line(): whole = lax.dynamic_update_index_in_dim(whole, taken, (z - k) % n, 0)  22 us
    dot_general x13, matrix products, dims(): lax.dot_general(left, right, (((left_axis,), (right_axis,)), ((), ())), p...  21.3 us
    ppermute x15, starting transfers between devices, swap_y(): return lax.ppermute(value, 'gx', [(i, i ^ 1) for i in range(self.nx)])  20.3 us
    ppermute x9, waiting for transfers between devices, swap_x(): return lax.ppermute(value, 'gy', [(i, i ^ 2) for i in range(self.ny)])  18.2 us
    unnamed x225, local copies, waits for them, and re-layouts  15.5 us
    ppermute x15, waiting for transfers between devices, swap_y(): return lax.ppermute(value, 'gx', [(i, i ^ 1) for i in range(self.nx)])  14.4 us
  transfers between devices with their start and end apart: 90, of which 23 were waited for; matrix products, arithmetic and copies ran while one was open for 35% of the time, Pallas kernels for 2%

profile of v1, /device:TPU:0, one launch (start us, length us, event | category | flops | bytes accessed | tf_op | source)
XLA Modules:
  0.0 537.1 jit_solution(7117368404891419467)
XLA Ops:
  25.9 5.2 collective-permute-start.16
  59.3 9.0 %collective-permute-done.3 = bf16[384,384]{0,1:T(8,128)(2,1)} collective-permute-done((bf16[384,384]{0,1:T(8,128)(2,1)S(1)}, bf16[384,384]{0,1:T(8,128)(2,1)}, u32[]{:S(2)}, u32[]{:S(2)}) %collective-permute-start.3) | collective-permute-done | bytes 294944 | tf_op jit(solution)/shard_map/ppermute | solution.py:52
  70.8 6.0 %collective-permute-start.36 = (bf16[384,512]{1,0:T(8,128)(2,1)}, bf16[384,512]{1,0:T(8,128)(2,1)}, u32[]{:S(2)}, u32[]{:S(2)}) collective-permute-start(bf16[384,512]{1,0:T(8,128)(2,1)} %pad_maximum_fusion.18), channel_id=1, source_target_pairs={{0,8},{4,12},{8,16},{12,20},{16,24},{20,28},{1,9},{5,13},{9,17},{1... | collective-permute-start | bytes 1179656 | tf_op jit(solution)/shard_map/ppermute | solution.py:52
  96.6 4.8 convert_element_type.606
  104.3 5.2 collective-permute-start.12
  116.1 6.7 %collective-permute-start.29 = (bf16[384,1024]{1,0:T(8,128)(2,1)}, bf16[384,1024]{1,0:T(8,128)(2,1)}, u32[]{:S(2)}, u32[]{:S(2)}) collective-permute-start(bf16[384,1024]{1,0:T(8,128)(2,1)} %pad_maximum_fusion.5), channel_id=1, source_target_pairs={{0,8},{4,12},{8,16},{12,20},{16,24},{20,28},{1,9},{5,13},{9,17},{1... | collective-permute-start | bytes 2359304 | tf_op jit(solution)/shard_map/ppermute | solution.py:52
  127.0 6.6 %dynamic_update_slice.57 = bf16[4,384,192]{1,0,2:T(4,128)(2,1)} dynamic-update-slice(bf16[4,384,192]{1,0,2:T(4,128)(2,1)} %copy-done.33, bf16[1,384,192]{1,0,2:T(2,128)(2,1)} %copy.95, s32[]{:T(128)S(6)} %select_n.707, s32[]{:T(128)} %constant.216.clone.1, s32[]{:T(128)} %constant.216.clone.1) | dynamic-update-slice | bytes 294916 | tf_op jit(solution)/shard_map/jit(dynamic_update_index_in_dim)/dynamic_update_slice | solution.py:77
  133.6 6.6 %dynamic_update_slice.58 = bf16[4,384,192]{1,0,2:T(4,128)(2,1)} dynamic-update-slice(bf16[4,384,192]{1,0,2:T(4,128)(2,1)} %dynamic_update_slice.57, bf16[1,384,192]{1,0,2:T(2,128)(2,1)} %copy.96, s32[]{:T(128)S(6)} %select_n.711, s32[]{:T(128)} %constant.216.clone.1, s32[]{:T(128)} %constant.216.clone.1) | dynamic-update-slice | bytes 294916 | tf_op jit(solution)/shard_map/jit(dynamic_update_index_in_dim)/dynamic_update_slice | solution.py:77
  140.2 6.6 %dynamic_update_slice.59 = bf16[4,384,192]{1,0,2:T(4,128)(2,1)} dynamic-update-slice(bf16[4,384,192]{1,0,2:T(4,128)(2,1)} %dynamic_update_slice.58, bf16[1,384,192]{1,0,2:T(2,128)(2,1)} %copy.97, s32[]{:T(128)S(6)} %select_n.715, s32[]{:T(128)} %constant.216.clone.1, s32[]{:T(128)} %constant.216.clone.1) | dynamic-update-slice | bytes 294916 | tf_op jit(solution)/shard_map/jit(dynamic_update_index_in_dim)/dynamic_update_slice | solution.py:77
  154.0 5.3 shard_map.194
  175.1 8.5 %collective-permute-done.39 = bf16[384,512]{1,0:T(8,128)(2,1)} collective-permute-done((bf16[384,512]{1,0:T(8,128)(2,1)}, bf16[384,512]{1,0:T(8,128)(2,1)}, u32[]{:S(2)}, u32[]{:S(2)}) %collective-permute-start.39) | collective-permute-done | bytes 393248 | tf_op jit(solution)/shard_map/ppermute | solution.py:52
  190.5 10.9 %collective-permute-done.31 = bf16[384,1024]{1,0:T(8,128)(2,1)} collective-permute-done((bf16[384,1024]{1,0:T(8,128)(2,1)}, bf16[384,1024]{1,0:T(8,128)(2,1)}, u32[]{:S(2)}, u32[]{:S(2)}) %collective-permute-start.31) | collective-permute-done | bytes 786464 | tf_op jit(solution)/shard_map/ppermute | solution.py:52
  212.9 5.2 squeeze.103
  218.1 6.0 %copy.108 = f32[1,2,256,2,2,384]{5,4,3,2,1,0:T(2,128)} copy(f32[1,2,256,2,2,384]{5,2,0,3,1,4:T(8,128)} %get-tuple-element.77) | data formatting | bytes 6291456 | tf_op jit(solution)/shard_map/convert_element_type | solution.py:333
  224.1 5.5 %reshape.553 = f32[512,1536]{1,0:T(8,128)} reshape(f32[1,2,256,2,2,384]{5,4,3,2,1,0:T(2,128)} %copy.108) | data formatting | bytes 6291456 | tf_op jit(solution)/shard_map/convert_element_type | solution.py:333
  247.7 5.3 reshape.540
  259.5 4.8 convert_element_type.629
  272.9 6.1 %collective-permute-start.86 = (bf16[384,512]{1,0:T(8,128)(2,1)S(1)}, bf16[384,512]{1,0:T(8,128)(2,1)S(1)}, u32[]{:S(2)}, u32[]{:S(2)}) collective-permute-start(bf16[384,512]{1,0:T(8,128)(2,1)S(1)} %get-tuple-element.95), channel_id=1, source_target_pairs={{0,8},{4,12},{1,9},{5,13},{2,10},{6,14},{3,11},{7,15}} | collective-permute-start | bytes 1179656 | tf_op jit(solution)/shard_map/ppermute | solution.py:52
  287.7 22.3 %collective-permute-start.87 = (bf16[384,512]{1,0:T(8,128)(2,1)S(1)}, bf16[384,512]{1,0:T(8,128)(2,1)S(1)}, u32[]{:S(2)}, u32[]{:S(2)}) collective-permute-start(bf16[384,512]{1,0:T(8,128)(2,1)S(1)} %get-tuple-element.93), channel_id=1, source_target_pairs={{0,8},{4,12},{8,16},{12,20},{1,9},{5,13},{9,17},{13,21},{2,10},{6,... | collective-permute-start | bytes 1179656 | tf_op jit(solution)/shard_map/ppermute | solution.py:52
  314.7 9.0 %collective-permute-done.46 = bf16[512,384]{1,0:T(8,128)(2,1)S(1)} collective-permute-done((bf16[512,384]{1,0:T(8,128)(2,1)S(1)}, bf16[512,384]{1,0:T(8,128)(2,1)S(1)}, u32[]{:S(2)}, u32[]{:S(2)}) %collective-permute-start.46) | collective-permute-done | bytes 393248 | tf_op jit(solution)/shard_map/ppermute | solution.py:45
  325.4 4.6 collective-permute-start.88
  332.4 5.3 collective-permute-done.49
  342.1 5.0 collective-permute-done.89
  350.6 5.1 reshape.545
  374.6 6.6 %shard_map.195 = (f32[2,96,512]{2,1,0:T(8,128)}, f32[192,512]{1,0:T(8,128)}, f32[192,1024]{1,0:T(8,128)}) custom-call(s32[2]{0:T(128)} %get-tuple-element.201.refs_0_, bf16[2,96,512]{2,1,0:T(8,128)(2,1)} %fusion.61.refs_1_, bf16[192,512]{1,0:T(8,128)(2,1)} %copy-done.34, bf16[192,1024]{1,0:T(8,128)(2,1)} %pad_maximum_fusion.15.refs_3_, ...), custom_call_target="tpu_custom_call" | custom-call | tf_op jit(solution)/shard_map/pallas_call | solution.py:277
  394.6 5.0 collective-permute-start.66
  399.7 12.9 %collective-permute-start.79 = (bf16[384,1024]{1,0:T(8,128)(2,1)}, bf16[384,1024]{1,0:T(8,128)(2,1)}, u32[]{:S(2)}, u32[]{:S(2)}) collective-permute-start(bf16[384,1024]{1,0:T(8,128)(2,1)} %get-tuple-element.76), channel_id=1, source_target_pairs={{0,8},{4,12},{1,9},{5,13},{2,10},{6,14},{3,11},{7,15}} | collective-permute-start | bytes 2359304 | tf_op jit(solution)/shard_map/ppermute | solution.py:52
  416.5 5.7 %collective-permute-done.53 = bf16[192,512]{1,0:T(8,128)(2,1)S(1)} collective-permute-done((bf16[192,512]{1,0:T(8,128)(2,1)S(1)}, bf16[192,512]{1,0:T(8,128)(2,1)S(1)}, u32[]{:S(2)}, u32[]{:S(2)}) %collective-permute-start.53) | collective-permute-done | bytes 196640 | tf_op jit(solution)/shard_map/ppermute | solution.py:52
  474.0 15.6 %collective-permute-start.80 = (bf16[384,1024]{1,0:T(8,128)(2,1)S(1)}, bf16[384,1024]{1,0:T(8,128)(2,1)S(1)}, u32[]{:S(2)}, u32[]{:S(2)}) collective-permute-start(bf16[384,1024]{1,0:T(8,128)(2,1)S(1)} %get-tuple-element.74), channel_id=1, source_target_pairs={{0,8},{4,12},{8,16},{12,20},{1,9},{5,13},{9,17},{13,21},{2,10},{6,... | collective-permute-start | bytes 2359304 | tf_op jit(solution)/shard_map/ppermute | solution.py:52
  498.9 5.3 collective-permute-done.80
  504.4 5.3 collective-permute-start.81
  515.0 7.7 %collective-permute-done.60 = f32[2,384]{1,0:T(2,128)S(1)} collective-permute-done((f32[2,384]{1,0:T(2,128)S(1)}, f32[2,384]{1,0:T(2,128)S(1)}, u32[]{:S(2)}, u32[]{:S(2)}) %collective-permute-start.60) | collective-permute-done | bytes 3104 | tf_op jit(solution)/shard_map/ppermute | solution.py:42
  (601 shorter events, 303.7 us)
Async XLA Ops:
  14.2 35.4 %collective-permute-start.35 = (bf16[192,512]{1,0:T(8,128)(2,1)}, bf16[192,512]{1,0:T(8,128)(2,1)}, u32[]{:S(2)}, u32[]{:S(2)}) collective-permute-start(bf16[192,512]{1,0:T(8,128)(2,1)} %broadcast_select_fusion.10), channel_id=1, source_target_pairs={{0,4},{4,0},{8,12},{12,8},{16,20},{20,16},{24,28},{28,24},{1,5},{5... | collective-permute-start | bytes 589832 | tf_op jit(solution)/shard_map/ppermute | solution.py:39
  22.5 23.0 %collective-permute-start.8 = (bf16[2,2,256,384]{3,2,1,0:T(8,128)(2,1)}, bf16[2,2,256,384]{3,2,1,0:T(8,128)(2,1)}, u32[]{:S(2)}, u32[]{:S(2)}) collective-permute-start(bf16[2,2,256,384]{3,2,1,0:T(8,128)(2,1)} %pad_maximum_fusion.2), channel_id=1, source_target_pairs={{0,4},{4,0},{8,12},{12,8},{16,20},{20,16},{24,28},{28,24},{1,5},{5... | collective-permute-start | bytes 2359304 | tf_op jit(solution)/shard_map/ppermute | solution.py:39
  49.6 38.6 %collective-permute-start.9 = (bf16[2,2,2,256,384]{4,3,2,1,0:T(8,128)(2,1)}, bf16[2,2,2,256,384]{4,3,2,1,0:T(8,128)(2,1)}, u32[]{:S(2)}, u32[]{:S(2)}) collective-permute-start(bf16[2,2,2,256,384]{4,3,2,1,0:T(8,128)(2,1)} %pad_maximum_fusion), channel_id=1, source_target_pairs={{0,1},{1,0},{2,3},{3,2},{4,5},{5,4},{6,7},{7,6},{8,9},{9,8},{10,11... | collective-permute-start | bytes 4718600 | tf_op jit(solution)/shard_map/ppermute | solution.py:48
  53.2 51.2 %collective-permute-start.28 = (bf16[192,1024]{1,0:T(8,128)(2,1)}, bf16[192,1024]{1,0:T(8,128)(2,1)}, u32[]{:S(2)}, u32[]{:S(2)}) collective-permute-start(bf16[192,1024]{1,0:T(8,128)(2,1)} %pad_maximum_fusion.17), channel_id=1, source_target_pairs={{0,4},{4,0},{8,12},{12,8},{16,20},{20,16},{24,28},{28,24},{1,5},{5... | collective-permute-start | bytes 1179656 | tf_op jit(solution)/shard_map/ppermute | solution.py:39
  54.7 94.2 %collective-permute-start.37 = (bf16[384,512]{1,0:T(8,128)(2,1)}, bf16[384,512]{1,0:T(8,128)(2,1)}, u32[]{:S(2)}, u32[]{:S(2)}) collective-permute-start(bf16[384,512]{1,0:T(8,128)(2,1)} %pad_maximum_fusion.18), channel_id=1, source_target_pairs={{8,0},{12,4},{16,8},{20,12},{24,16},{28,20},{9,1},{13,5},{17,9},{2... | collective-permute-start | bytes 1179656 | tf_op jit(solution)/shard_map/ppermute | solution.py:52
  70.8 93.9 %collective-permute-start.36 = (bf16[384,512]{1,0:T(8,128)(2,1)}, bf16[384,512]{1,0:T(8,128)(2,1)}, u32[]{:S(2)}, u32[]{:S(2)}) collective-permute-start(bf16[384,512]{1,0:T(8,128)(2,1)} %pad_maximum_fusion.18), channel_id=1, source_target_pairs={{0,8},{4,12},{8,16},{12,20},{16,24},{20,28},{1,9},{5,13},{9,17},{1... | collective-permute-start | bytes 1179656 | tf_op jit(solution)/shard_map/ppermute | solution.py:52
  82.8 29.7 %collective-permute-start.19 = (bf16[384,192]{0,1:T(8,128)(2,1)}, bf16[384,192]{0,1:T(8,128)(2,1)}, u32[]{:S(2)}, u32[]{:S(2)}) collective-permute-start(bf16[384,192]{0,1:T(8,128)(2,1)} %collective-permute-done.18), channel_id=1, source_target_pairs={{8,0},{12,4},{9,1},{13,5},{10,2},{14,6},{11,3},{15,7}} | collective-permute-start | bytes 442376 | tf_op jit(solution)/shard_map/ppermute | solution.py:52
  88.1 28.0 %collective-permute-start.21 = (bf16[384,192]{0,1:T(8,128)(2,1)}, bf16[384,192]{0,1:T(8,128)(2,1)}, u32[]{:S(2)}, u32[]{:S(2)}) collective-permute-start(bf16[384,192]{0,1:T(8,128)(2,1)} %collective-permute-done.20), channel_id=1, source_target_pairs={{16,24},{20,28},{17,25},{21,29},{18,26},{22,30},{19,27},{23,31}} | collective-permute-start | bytes 442376 | tf_op jit(solution)/shard_map/ppermute | solution.py:52
  112.5 59.7 %collective-permute-start.30 = (bf16[384,1024]{1,0:T(8,128)(2,1)}, bf16[384,1024]{1,0:T(8,128)(2,1)}, u32[]{:S(2)}, u32[]{:S(2)}) collective-permute-start(bf16[384,1024]{1,0:T(8,128)(2,1)} %pad_maximum_fusion.5), channel_id=1, source_target_pairs={{8,0},{12,4},{16,8},{20,12},{24,16},{28,20},{9,1},{13,5},{17,9},{2... | collective-permute-start | bytes 2359304 | tf_op jit(solution)/shard_map/ppermute | solution.py:52
  116.1 57.4 %collective-permute-start.29 = (bf16[384,1024]{1,0:T(8,128)(2,1)}, bf16[384,1024]{1,0:T(8,128)(2,1)}, u32[]{:S(2)}, u32[]{:S(2)}) collective-permute-start(bf16[384,1024]{1,0:T(8,128)(2,1)} %pad_maximum_fusion.5), channel_id=1, source_target_pairs={{0,8},{4,12},{8,16},{12,20},{16,24},{20,28},{1,9},{5,13},{9,17},{1... | collective-permute-start | bytes 2359304 | tf_op jit(solution)/shard_map/ppermute | solution.py:52
  122.8 29.3 %collective-permute-start.14 = (bf16[192,512]{1,0:T(8,128)(2,1)}, bf16[192,512]{1,0:T(8,128)(2,1)}, u32[]{:S(2)}, u32[]{:S(2)}) collective-permute-start(bf16[192,512]{1,0:T(8,128)(2,1)} %collective-permute-done.13), channel_id=1, source_target_pairs={{16,24},{20,28},{17,25},{21,29},{18,26},{22,30},{19,27},{23,31}} | collective-permute-start | bytes 589832 | tf_op jit(solution)/shard_map/ppermute | solution.py:52
  164.7 20.0 %collective-permute-start.22 = (bf16[2,512,384]{2,1,0:T(8,128)(2,1)}, bf16[2,512,384]{2,1,0:T(8,128)(2,1)}, u32[]{:S(2)}, u32[]{:S(2)}) collective-permute-start(bf16[2,512,384]{2,1,0:T(8,128)(2,1)} %pad_maximum_fusion.3), channel_id=1, source_target_pairs={{0,1},{1,0},{2,3},{3,2},{4,5},{5,4},{6,7},{7,6},{8,9},{9,8},{10,11... | collective-permute-start | bytes 2359304 | tf_op jit(solution)/shard_map/ppermute | solution.py:48
  172.2 29.2 %collective-permute-start.31 = (bf16[384,1024]{1,0:T(8,128)(2,1)}, bf16[384,1024]{1,0:T(8,128)(2,1)}, u32[]{:S(2)}, u32[]{:S(2)}) collective-permute-start(bf16[384,1024]{1,0:T(8,128)(2,1)} %collective-permute-done.30), channel_id=1, source_target_pairs={{8,0},{12,4},{16,8},{20,12},{9,1},{13,5},{17,9},{21,13},{10,2},{14... | collective-permute-start | bytes 2359304 | tf_op jit(solution)/shard_map/ppermute | solution.py:52
  173.6 29.2 %collective-permute-start.33 = (bf16[384,1024]{1,0:T(8,128)(2,1)}, bf16[384,1024]{1,0:T(8,128)(2,1)}, u32[]{:S(2)}, u32[]{:S(2)}) collective-permute-start(bf16[384,1024]{1,0:T(8,128)(2,1)} %collective-permute-done.29), channel_id=1, source_target_pairs={{8,16},{12,20},{16,24},{20,28},{9,17},{13,21},{17,25},{21,29},{10,... | collective-permute-start | bytes 2359304 | tf_op jit(solution)/shard_map/ppermute | solution.py:52
  201.4 32.2 %collective-permute-start.32 = (bf16[384,1024]{1,0:T(8,128)(2,1)}, bf16[384,1024]{1,0:T(8,128)(2,1)}, u32[]{:S(2)}, u32[]{:S(2)}) collective-permute-start(bf16[384,1024]{1,0:T(8,128)(2,1)} %collective-permute-done.31), channel_id=1, source_target_pairs={{8,0},{12,4},{9,1},{13,5},{10,2},{14,6},{11,3},{15,7}} | collective-permute-start | bytes 2359304 | tf_op jit(solution)/shard_map/ppermute | solution.py:52
  202.7 39.2 %collective-permute-start.34 = (bf16[384,1024]{1,0:T(8,128)(2,1)}, bf16[384,1024]{1,0:T(8,128)(2,1)}, u32[]{:S(2)}, u32[]{:S(2)}) collective-permute-start(bf16[384,1024]{1,0:T(8,128)(2,1)} %collective-permute-done.33), channel_id=1, source_target_pairs={{16,24},{20,28},{17,25},{21,29},{18,26},{22,30},{19,27},{23,31}} | collective-permute-start | bytes 2359304 | tf_op jit(solution)/shard_map/ppermute | solution.py:52
  205.1 30.8 %collective-permute-start.26 = (bf16[512,384]{1,0:T(8,128)(2,1)}, bf16[512,384]{1,0:T(8,128)(2,1)}, u32[]{:S(2)}, u32[]{:S(2)}) collective-permute-start(bf16[512,384]{1,0:T(8,128)(2,1)} %fusion.21), channel_id=1, source_target_pairs={{0,2},{1,3},{2,0},{3,1},{4,6},{5,7},{6,4},{7,5},{8,10},{9,11},{10,... | collective-permute-start | bytes 1179656 | tf_op jit(solution)/shard_map/ppermute | solution.py:45
  207.5 28.5 %collective-permute-start.24 = (bf16[512,384]{1,0:T(8,128)(2,1)}, bf16[512,384]{1,0:T(8,128)(2,1)}, u32[]{:S(2)}, u32[]{:S(2)}) collective-permute-start(bf16[512,384]{1,0:T(8,128)(2,1)} %fusion.20), channel_id=1, source_target_pairs={{0,4},{4,0},{8,12},{12,8},{16,20},{20,16},{24,28},{28,24},{1,5},{5... | collective-permute-start | bytes 1179656 | tf_op jit(solution)/shard_map/ppermute | solution.py:39
  281.5 30.6 %collective-permute-start.42 = (bf16[2,512,384]{2,1,0:T(8,128)(2,1)S(1)}, bf16[2,512,384]{2,1,0:T(8,128)(2,1)S(1)}, u32[]{:S(2)}, u32[]{:S(2)}) collective-permute-start(bf16[2,512,384]{2,1,0:T(8,128)(2,1)S(1)} %pad_maximum_fusion.6), channel_id=1, source_target_pairs={{0,1},{1,0},{2,3},{3,2},{4,5},{5,4},{6,7},{7,6},{8,9},{9,8},{10,11... | collective-permute-start | bytes 2359304 | tf_op jit(solution)/shard_map/ppermute | solution.py:48
  283.8 30.1 %collective-permute-start.48 = (bf16[512,384]{1,0:T(8,128)(2,1)S(1)}, bf16[512,384]{1,0:T(8,128)(2,1)S(1)}, u32[]{:S(2)}, u32[]{:S(2)}) collective-permute-start(bf16[512,384]{1,0:T(8,128)(2,1)S(1)} %get-tuple-element.63), channel_id=1, source_target_pairs={{0,4},{4,0},{8,12},{12,8},{16,20},{20,16},{24,28},{28,24},{1,5},{5... | collective-permute-start | bytes 1179656 | tf_op jit(solution)/shard_map/ppermute | solution.py:39
  287.7 37.6 %collective-permute-start.87 = (bf16[384,512]{1,0:T(8,128)(2,1)S(1)}, bf16[384,512]{1,0:T(8,128)(2,1)S(1)}, u32[]{:S(2)}, u32[]{:S(2)}) collective-permute-start(bf16[384,512]{1,0:T(8,128)(2,1)S(1)} %get-tuple-element.93), channel_id=1, source_target_pairs={{0,8},{4,12},{8,16},{12,20},{1,9},{5,13},{9,17},{13,21},{2,10},{6,... | collective-permute-start | bytes 1179656 | tf_op jit(solution)/shard_map/ppermute | solution.py:52
  310.0 29.1 %collective-permute-start.85 = (bf16[384,512]{1,0:T(8,128)(2,1)S(1)}, bf16[384,512]{1,0:T(8,128)(2,1)S(1)}, u32[]{:S(2)}, u32[]{:S(2)}) collective-permute-start(bf16[384,512]{1,0:T(8,128)(2,1)S(1)} %get-tuple-element.92), channel_id=1, source_target_pairs={{8,0},{12,4},{16,8},{20,12},{24,16},{28,20},{9,1},{13,5},{17,9},{2... | collective-permute-start | bytes 1179656 | tf_op jit(solution)/shard_map/ppermute | solution.py:52
  314.1 23.6 %collective-permute-start.49 = (bf16[512,384]{1,0:T(8,128)(2,1)S(1)}, bf16[512,384]{1,0:T(8,128)(2,1)S(1)}, u32[]{:S(2)}, u32[]{:S(2)}) collective-permute-start(bf16[512,384]{1,0:T(8,128)(2,1)S(1)} %fusion.23), channel_id=1, source_target_pairs={{0,2},{1,3},{2,0},{3,1},{4,6},{5,7},{6,4},{7,5},{8,10},{9,11},{10,... | collective-permute-start | bytes 1179656 | tf_op jit(solution)/shard_map/ppermute | solution.py:45
  341.6 186.8 %collective-permute-start.44 = (bf16[256,384]{1,0:T(8,128)(2,1)}, bf16[256,384]{1,0:T(8,128)(2,1)}, u32[]{:S(2)}, u32[]{:S(2)}) collective-permute-start(bf16[256,384]{1,0:T(8,128)(2,1)} %select_convert_fusion.15), channel_id=1, source_target_pairs={{0,4},{4,0},{8,12},{12,8},{16,20},{20,16},{24,28},{28,24},{1,5},{5... | collective-permute-start | bytes 589832 | tf_op jit(solution)/shard_map/ppermute | solution.py:39
  364.7 76.3 %collective-permute-start.76 = (bf16[384,1024]{1,0:T(8,128)(2,1)}, bf16[384,1024]{1,0:T(8,128)(2,1)}, u32[]{:S(2)}, u32[]{:S(2)}) collective-permute-start(bf16[384,1024]{1,0:T(8,128)(2,1)} %get-tuple-element.75), channel_id=1, source_target_pairs={{24,16},{28,20},{25,17},{29,21},{26,18},{30,22},{27,19},{31,23}} | collective-permute-start | bytes 2359304 | tf_op jit(solution)/shard_map/ppermute | solution.py:52
  399.7 71.6 %collective-permute-start.79 = (bf16[384,1024]{1,0:T(8,128)(2,1)}, bf16[384,1024]{1,0:T(8,128)(2,1)}, u32[]{:S(2)}, u32[]{:S(2)}) collective-permute-start(bf16[384,1024]{1,0:T(8,128)(2,1)} %get-tuple-element.76), channel_id=1, source_target_pairs={{0,8},{4,12},{1,9},{5,13},{2,10},{6,14},{3,11},{7,15}} | collective-permute-start | bytes 2359304 | tf_op jit(solution)/shard_map/ppermute | solution.py:52
  414.9 28.8 %collective-permute-start.64 = (bf16[384,384]{0,1:T(8,128)(2,1)}, bf16[384,384]{0,1:T(8,128)(2,1)}, u32[]{:S(2)}, u32[]{:S(2)}) collective-permute-start(bf16[384,384]{0,1:T(8,128)(2,1)} %get-tuple-element.112), channel_id=1, source_target_pairs={{8,0},{12,4},{16,8},{20,12},{24,16},{28,20},{9,1},{13,5},{17,9},{2... | collective-permute-start | bytes 884744 | tf_op jit(solution)/shard_map/ppermute | solution.py:52
  441.0 27.1 %collective-permute-start.54 = (bf16[2,512,384]{2,1,0:T(8,128)(2,1)}, bf16[2,512,384]{2,1,0:T(8,128)(2,1)}, u32[]{:S(2)}, u32[]{:S(2)}) collective-permute-start(bf16[2,512,384]{2,1,0:T(8,128)(2,1)} %pad_maximum_fusion.9), channel_id=1, source_target_pairs={{0,1},{1,0},{2,3},{3,2},{4,5},{5,4},{6,7},{7,6},{8,9},{9,8},{10,11... | collective-permute-start | bytes 2359304 | tf_op jit(solution)/shard_map/ppermute | solution.py:48
  469.5 20.2 %collective-permute-start.55 = (bf16[512,384]{1,0:T(8,128)(2,1)S(1)}, bf16[512,384]{1,0:T(8,128)(2,1)S(1)}, u32[]{:S(2)}, u32[]{:S(2)}) collective-permute-start(bf16[512,384]{1,0:T(8,128)(2,1)S(1)} %select_convert_fusion.1), channel_id=1, source_target_pairs={{0,2},{1,3},{2,0},{3,1},{4,6},{5,7},{6,4},{7,5},{8,10},{9,11},{10,... | collective-permute-start | bytes 1179656 | tf_op jit(solution)/shard_map/ppermute | solution.py:45
  474.0 30.1 %collective-permute-start.80 = (bf16[384,1024]{1,0:T(8,128)(2,1)S(1)}, bf16[384,1024]{1,0:T(8,128)(2,1)S(1)}, u32[]{:S(2)}, u32[]{:S(2)}) collective-permute-start(bf16[384,1024]{1,0:T(8,128)(2,1)S(1)} %get-tuple-element.74), channel_id=1, source_target_pairs={{0,8},{4,12},{8,16},{12,20},{1,9},{5,13},{9,17},{13,21},{2,10},{6,... | collective-permute-start | bytes 2359304 | tf_op jit(solution)/shard_map/ppermute | solution.py:52
  492.8 32.0 %collective-permute-start.78 = (bf16[384,1024]{1,0:T(8,128)(2,1)}, bf16[384,1024]{1,0:T(8,128)(2,1)}, u32[]{:S(2)}, u32[]{:S(2)}) collective-permute-start(bf16[384,1024]{1,0:T(8,128)(2,1)} %get-tuple-element.73), channel_id=1, source_target_pairs={{8,0},{12,4},{16,8},{20,12},{24,16},{28,20},{9,1},{13,5},{17,9},{2... | collective-permute-start | bytes 2359304 | tf_op jit(solution)/shard_map/ppermute | solution.py:52
  504.4 20.3 %collective-permute-start.81 = (bf16[384,1024]{1,0:T(8,128)(2,1)S(1)}, bf16[384,1024]{1,0:T(8,128)(2,1)}, u32[]{:S(2)}, u32[]{:S(2)}) collective-permute-start(bf16[384,1024]{1,0:T(8,128)(2,1)S(1)} %fusion.1), channel_id=1, source_target_pairs={{0,8},{4,12},{8,16},{12,20},{16,24},{20,28},{1,9},{5,13},{9,17},{1... | collective-permute-start | bytes 2359304 | tf_op jit(solution)/shard_map/ppermute | solution.py:52
  (161 other events, 1313.6 us)
